TPU v7x, 32 devices: a whole 2x2x4 slice. The times are simulated.
32 devices in a mesh: wave: 2 (over y), ty: 4 (over z), tx: 4 (over x, core).
Axes of the slice: x: 2, y: 2, z: 4, core: 2. Of those that a mesh axis runs over, the one named last changes fastest.
Arguments:
- object_field: float32 [2, 2048, 2048], P(None, 'ty', 'tx'), may hold values from -5 to 5
- probes: float32 [2, 2, 256, 256], P('wave'), may hold values from -5 to 5
- measured: float32 [4, 4, 8, 256, 256], P('ty', 'tx'), may hold values from 0.1 to 4
- positions: int32 [4, 4, 8, 2], P('ty', 'tx'), may hold values from 0 to 256, as said below
- weights: float32 [2], P('wave'), may hold values from 0.5 to 12, as said below
Outputs:
- new_object: float32 [2, 2048, 2048], P(None, 'ty', 'tx')
- new_probes: float32 [2, 2, 256, 256], P('wave')
Inputs may be any that keep to these rules, and one draw needn't show every extreme that they name: `positions`: each frame lies wholly inside its tile; some offset equals 0 and some equals 256. Positive weights.
All inputs are finite; a program needn't handle non-finite values.
Results may differ from a plain program's by a relative error of at most 0.0003.
Values sent between devices are 32-bit elements; how exact they have to be, the bound alone decides.
A program may use at most 64 MiB of HBM per device.

v0:
```python
import functools
import math

import jax
import jax.numpy as jnp
import numpy as np
from jax import lax
from jax.experimental import pallas as pl
from jax.experimental.pallas import tpu as pltpu
from jax.sharding import PartitionSpec as P

damping = 1.0
intensity_offset = 0.1


def tables(length):
    indices = np.arange(length)
    angles = 2.0 * math.pi / length * (indices[:, None] * indices[None, :] % length)
    cosine = np.cos(angles) / math.sqrt(length)
    sine = -np.sin(angles) / math.sqrt(length)
    right = []
    for table in (cosine, sine - cosine, sine + cosine):
        high = table.astype(jnp.bfloat16)
        low = (table - high.astype(np.float64)).astype(jnp.bfloat16)
        right.append(np.concatenate([high, high, low], axis=0))
    right = np.stack(right)
    return right, np.ascontiguousarray(right.transpose(0, 2, 1))


def split(x):
    high = x.astype(jnp.bfloat16)
    low = (x - high.astype(jnp.float32)).astype(jnp.bfloat16)
    return high, low


def times_right(x, table):
    high, low = split(x)
    return jnp.dot(
        jnp.concatenate([high, low, high], axis=1), table, preferred_element_type=jnp.float32
    )


def times_left(x, table):
    high, low = split(x)
    return jnp.dot(
        table, jnp.concatenate([high, low, high], axis=0), preferred_element_type=jnp.float32
    )


def forward(real, imag, right, left):
    for times, table in ((times_right, right), (times_left, left)):
        both = times(real + imag, table[0])
        real, imag = both - times(imag, table[2]), both + times(real, table[1])
    return real, imag


def inverse(real, imag, right, left):
    for times, table in ((times_right, right), (times_left, left)):
        both = times(real + imag, table[0])
        real, imag = both + times(imag, table[1]), both - times(real, table[2])
    return real, imag


def step_kernel(
    pos, wts, obj, probes, meas, right, left, new_obj, q, e, patch, psi, hacc, light, grad, power
):
    waves = probes.shape[0]
    count = meas.shape[0]
    psize = probes.shape[-1]
    side = obj.shape[-1]
    tall = psize + 8
    total = wts[0]
    for w in range(1, waves):
        total = total + wts[w]
    inv_total = 1.0 / jnp.full((1, psize), total)
    light[...] = probes[0, 0] * probes[0, 0] + probes[0, 1] * probes[0, 1]

    def each_wave(start, body):
        if waves - start <= 2:
            for w in range(start, waves):
                body(w)
        else:
            pl.loop(start, waves)(body)

    def add_light(w):
        light[...] += probes[w, 0] * probes[w, 0] + probes[w, 1] * probes[w, 1]

    each_wave(1, add_light)
    new_obj[...] = jnp.zeros_like(new_obj)
    hacc[...] = jnp.zeros_like(hacc)
    q[...] = jnp.zeros_like(q)
    e[...] = jnp.zeros_like(e)

    @pl.loop(0, count)
    def _(f):
        r, c = pos[f, 0], pos[f, 1]
        back = lax.rem(side - c, side)
        base = pl.multiple_of(jnp.minimum(r // 8 * 8, side - tall), 8)
        shift = r - base
        for ch in range(2):
            rows = pltpu.roll(obj[ch, pl.ds(base, tall), :], back, 1)[:, :psize]
            patch[ch] = pltpu.roll(rows, lax.rem(tall - shift, tall), 0)[:psize]
        e[...] += patch[0] * patch[0] + patch[1] * patch[1]
        power[...] = jnp.zeros_like(power)

        def far(w):
            pr, pi = probes[w, 0], probes[w, 1]
            o_r, o_i = patch[0], patch[1]
            real, imag = forward(pr * o_r - pi * o_i, pr * o_i + pi * o_r, right, left)
            psi[w, 0] = real
            psi[w, 1] = imag
            power[...] += wts[w] * (real * real + imag * imag)

        each_wave(0, far)
        power[...] = (
            jnp.sqrt(meas[f]) / jnp.sqrt(power[...] * inv_total + intensity_offset) - 1.0
        )
        grad[...] = jnp.zeros_like(grad)

        def near(w):
            factor = power[...]
            real, imag = inverse(psi[w, 0] * factor, psi[w, 1] * factor, right, left)
            pr, pi = probes[w, 0], probes[w, 1]
            grad[0] += pr * real + pi * imag
            grad[1] += pr * imag - pi * real
            if isinstance(w, int) and w == 0:
                o_r, o_i = patch[0], patch[1]
                q[0] += o_r * real + o_i * imag
                q[1] += o_r * imag - o_i * real

        near(0)
        each_wave(1, near)

        def place(window):
            below = jnp.zeros((tall - psize, psize), jnp.float32)
            window = pltpu.roll(jnp.concatenate([window, below], 0), shift, 0)
            beside = jnp.zeros((tall, side - psize), jnp.float32)
            return pltpu.roll(jnp.concatenate([window, beside], 1), c, 1)

        for ch in range(2):
            new_obj[ch, pl.ds(base, tall), :] += place(grad[ch])
        hacc[pl.ds(base, tall), :] += place(light[...])

    scale = 1.0 / (hacc[...] + damping)
    for ch in range(2):
        new_obj[ch] = obj[ch] + new_obj[ch] * scale


def local(waves, object_field, probes, measured, positions, weights):
    psize = probes.shape[-1]
    side = object_field.shape[-1]
    right, left = tables(psize)
    all_probes, all_weights = [probes], [weights]
    for turn in range(1, waves):
        ring = [(i, (i + turn) % waves) for i in range(waves)]
        all_probes.append(lax.ppermute(probes, "wave", ring))
        all_weights.append(lax.ppermute(weights, "wave", ring))
    all_probes = jnp.concatenate(all_probes)
    all_weights = jnp.concatenate(all_weights)
    vmem = pl.BlockSpec(memory_space=pltpu.VMEM)
    smem = pl.BlockSpec(memory_space=pltpu.SMEM)
    f32 = jnp.float32
    new_object, q, e = pl.pallas_call(
        step_kernel,
        out_shape=(
            jax.ShapeDtypeStruct(object_field.shape, f32),
            jax.ShapeDtypeStruct((2, psize, psize), f32),
            jax.ShapeDtypeStruct((psize, psize), f32),
        ),
        in_specs=[smem, smem] + [vmem] * 5,
        out_specs=(vmem,) * 3,
        scratch_shapes=[
            pltpu.VMEM((2, psize, psize), f32),
            pltpu.VMEM((waves, 2, psize, psize), f32),
            pltpu.VMEM((side, side), f32),
            pltpu.VMEM((psize, psize), f32),
            pltpu.VMEM((2, psize, psize), f32),
            pltpu.VMEM((psize, psize), f32),
        ],
        compiler_params=pltpu.CompilerParams(vmem_limit_bytes=60 * 2**20),
    )(positions[0, 0], all_weights, object_field, all_probes, measured[0, 0], right, left)
    q, e = lax.psum((q, e), ("ty", "tx"))
    new_probes = probes + (q / (e + damping))[None]
    return (new_object, new_probes)


def solution(mesh):
    in_specs = (
        P(None, "ty", "tx"),
        P("wave", None, None, None),
        P("ty", "tx", None, None, None),
        P("ty", "tx", None, None),
        P("wave"),
    )
    out_specs = (P(None, "ty", "tx"), P("wave", None, None, None))
    body = functools.partial(local, mesh.shape["wave"])
    return jax.shard_map(body, mesh=mesh, in_specs=in_specs, out_specs=out_specs, check_vma=False)
```

profile of v0, /device:TPU:0, one launch (start us, length us, event | category | flops | bytes accessed | tf_op | source)
XLA Modules:
  0.0 174.8 jit_solution(3002630694907755299)
XLA Ops:
  7.2 0.0 all-reduce.3.cloned.1.call-start
  7.2 3.1 %collective-permute-start.1 = (f32[1,2,256,256]{3,2,1,0:T(8,128)}, f32[1,2,256,256]{3,2,1,0:T(8,128)S(1)}, u32[]{:S(2)}, u32[]{:S(2)}) collective-permute-start(f32[1,2,256,256]{3,2,1,0:T(8,128)} %param.8), channel_id=1, source_target_pairs={{0,16},{16,0},{1,17},{17,1},{2,18},{18,2},{3,19},{19,3},{4,20},{20... | collective-permute-start | bytes 1572872 | tf_op jit(solution)/shard_map/ppermute | solution.py:156
  10.3 0.1 collective-permute-start
  11.0 1.3 copy.9.pos
  12.4 10.1 %collective-permute-done = f32[1]{0:T(128)} collective-permute-done((f32[1]{0:T(128)}, f32[1]{0:T(128)}, u32[]{:S(2)}, u32[]{:S(2)}) %collective-permute-start) | collective-permute-done | bytes 36 | tf_op jit(solution)/shard_map/ppermute | solution.py:157
  22.5 1.3 pad_maximum_fusion.1.wts
  23.7 0.0 collective-permute-done.1
  23.8 2.1 %pad_maximum_fusion.probes = f32[2,2,256,256]{3,2,1,0:T(8,128)} fusion(f32[1,2,256,256]{3,2,1,0:T(8,128)S(1)} %collective-permute-done.1, f32[1,2,256,256]{3,2,1,0:T(8,128)} %param.8), kind=kLoop, calls=%fused_computation | loop fusion | flops 262144 | bytes 2097152 | tf_op jit(solution)/shard_map/concatenate | solution.py:158
  25.9 0.0 copy-start
  25.9 44.7 %shard_map.86 = (f32[2,512,512]{2,1,0:T(8,128)}, f32[2,256,256]{2,1,0:T(8,128)}, f32[256,256]{1,0:T(8,128)}) custom-call(s32[8,2]{1,0:T(8,128)} %copy.9.pos, f32[2]{0:T(128)} %pad_maximum_fusion.1.wts, f32[2,512,512]{2,1,0:T(8,128)} %obj.1, f32[2,2,256,256]{3,2,1,0:T(8,128)} %pad_maximum_fusion.probes, f32[8,256,256]{2,1,0:T(8,128)} %bitcast.4, ...), custom_call_target="tpu_custom_call" | custom-call | tf_op jit(solution)/shard_map/pallas_call | solution.py:163
  70.5 0.0 all-reduce.3.cloned.1.call-update
  70.5 94.5 %all-reduce.3.cloned.1.call-done = (f32[2,256,256]{2,1,0:T(8,128)}, f32[256,256]{1,0:T(8,128)}) async-done(((f32[2,256,256]{2,1,0:T(8,128)}, f32[256,256]{1,0:T(8,128)}), (f32[2,256,256]{2,1,0:T(8,128)}, f32[256,256]{1,0:T(8,128)})) %all-reduce.3.cloned.1.call-update) | async-done | bytes 786448 | tf_op jit(solution)/shard_map/psum | solution.py:182
  165.1 1.0 broadcast_add_fusion
  166.0 0.0 copy-done
  166.0 1.9 %bitcast_add_fusion = f32[1,2,256,256]{3,2,1,0:T(8,128)} fusion(f32[1,2,256,256]{3,2,1,0:T(8,128)S(1)} %copy-done, f32[2,256,256]{2,1,0:T(8,128)} %get-tuple-element.8, f32[256,256]{1,0:T(8,128)S(1)} %broadcast_add_fusion), kind=kLoop, calls=%fused_computation.1 | loop fusion | flops 262144 | bytes 1835008 | tf_op jit(solution)/shard_map/add | solution.py:183
Async XLA Ops:
  7.2 157.9 %all-reduce.3.cloned.1.call-start = ((), (), s32[]{:S(2)}) async-start(), calls=%async_computation | async-start | bytes 1572864 | tf_op jit(solution)/shard_map/psum | solution.py:182
  7.2 16.5 %collective-permute-start.1 = (f32[1,2,256,256]{3,2,1,0:T(8,128)}, f32[1,2,256,256]{3,2,1,0:T(8,128)S(1)}, u32[]{:S(2)}, u32[]{:S(2)}) collective-permute-start(f32[1,2,256,256]{3,2,1,0:T(8,128)} %param.8), channel_id=1, source_target_pairs={{0,16},{16,0},{1,17},{17,1},{2,18},{18,2},{3,19},{19,3},{4,20},{20... | collective-permute-start | bytes 1572872 | tf_op jit(solution)/shard_map/ppermute | solution.py:156
  10.3 12.2 %collective-permute-start = (f32[1]{0:T(128)}, f32[1]{0:T(128)}, u32[]{:S(2)}, u32[]{:S(2)}) collective-permute-start(f32[1]{0:T(128)} %param.11), channel_id=1, source_target_pairs={{0,16},{16,0},{1,17},{17,1},{2,18},{18,2},{3,19},{19,3},{4,20},{20... | collective-permute-start | bytes 20 | tf_op jit(solution)/shard_map/ppermute | solution.py:157
  25.9 140.2 %copy-start = (f32[1,2,256,256]{3,2,1,0:T(8,128)S(1)}, f32[1,2,256,256]{3,2,1,0:T(8,128)}, u32[]{:S(2)}) copy-start(f32[1,2,256,256]{3,2,1,0:T(8,128)} %param.8) | copy-start | bytes 1572868
Sparse Core Ops, SparseCore 0:
  70.7 94.3 all-reduce.2
where the time goes:
time: 175 us
  waiting for transfers between devices  105 us (60%)
  Pallas kernels  44.7 us (26%)
  between operations  14.7 us (8%)
  other arithmetic  6.29 us (4%)
  starting transfers between devices  3.18 us (2%)
    psum x1, waiting for transfers between devices, local(): q, e = lax.psum((q, e), ('ty', 'tx'))  94.5 us
    pallas_call x1, Pallas kernels, local(): pl.pallas_call(step_kernel, out_shape=(jax.ShapeDtypeStruct(object_field....  44.7 us
    ppermute x1, waiting for transfers between devices, local(): all_weights.append(lax.ppermute(weights, 'wave', ring))  10.1 us
  transfers between devices with their start and end apart: 3, of which 2 were waited for; matrix products, arithmetic and copies ran while one was open for 2% of the time, Pallas kernels for 0%

commit v1 on v0

--- a/solution.py
+++ b/solution.py
@@ -184,6 +184,302 @@
     return (new_object, new_probes)
 
 
+def at(pos, f, side, tall):
+    r, c = pos[f, 0], pos[f, 1]
+    base = pl.multiple_of(jnp.minimum(r // 8 * 8, side - tall), 8)
+    return base, r - base, c
+
+
+def window_kernel(pos, obj, patch, e):
+    psize, side = patch.shape[-1], obj.shape[-1]
+    tall = psize + 8
+    f = pl.program_id(0)
+    base, shift, c = at(pos, f, side, tall)
+    power = jnp.zeros((psize, psize), jnp.float32)
+    for ch in range(2):
+        rows = pltpu.roll(obj[ch, pl.ds(base, tall), :], lax.rem(side - c, side), 1)[:, :psize]
+        rows = pltpu.roll(rows, lax.rem(tall - shift, tall), 0)[:psize]
+        patch[0, ch] = rows
+        power += rows * rows
+
+    @pl.when(f == 0)
+    def _():
+        e[0] = power
+
+    @pl.when(f > 0)
+    def _():
+        e[0] += power
+
+
+def scatter_kernel(pos, obj, grad, light, new_obj, hacc):
+    psize, side = grad.shape[-1], obj.shape[-1]
+    tall = psize + 8
+    f = pl.program_id(0)
+    base, shift, c = at(pos, f, side, tall)
+
+    @pl.when(f == 0)
+    def _():
+        new_obj[...] = jnp.zeros_like(new_obj)
+        hacc[...] = jnp.zeros_like(hacc)
+
+    def place(window):
+        below = jnp.zeros((tall - psize, psize), jnp.float32)
+        window = pltpu.roll(jnp.concatenate([window, below], 0), shift, 0)
+        beside = jnp.zeros((tall, side - psize), jnp.float32)
+        return pltpu.roll(jnp.concatenate([window, beside], 1), c, 1)
+
+    for ch in range(2):
+        new_obj[ch, pl.ds(base, tall), :] += place(grad[0, ch])
+    hacc[pl.ds(base, tall), :] += place(light[...])
+
+    @pl.when(f == pl.num_programs(0) - 1)
+    def _():
+        scale = 1.0 / (hacc[...] + damping)
+        for ch in range(2):
+            new_obj[ch] = obj[ch] + new_obj[ch] * scale
+
+
+def pair_kernel(
+    bits, rows_of_tiles,
+    wts, patch, e, probes, meas, right, left,
+    grad, light, new_probes,
+    other, wmine, wother, psi, q, q_sums, q_got, e_sums, e_got, q_pieces, e_pieces, result,
+    send, recv,
+):
+    count = meas.shape[0]
+    psize = probes.shape[-1]
+    f32 = jnp.float32
+    wave, ty, tx = lax.axis_index("wave"), lax.axis_index("ty"), lax.axis_index("tx")
+    mate = {"wave": 1 - wave}
+    halves = []
+    for bit in range(bits):
+        mine = tx // 2**bit % 2
+        halves.append((mine, {"tx": tx + (1 - 2 * mine) * 2**bit}))
+    others = [{"ty": lax.rem(ty + d, rows_of_tiles)} for d in range(1, rows_of_tiles)]
+
+    barrier = pltpu.get_barrier_semaphore()
+    partners = [mate] + [h[1] for h in halves] + others
+    for partner in partners:
+        pl.semaphore_signal(
+            barrier, inc=1, device_id=partner, device_id_type=pl.DeviceIdType.MESH
+        )
+    pl.semaphore_wait(barrier, len(partners))
+
+    used = [0]
+
+    def ship(src, dst, partner):
+        k = used[0]
+        used[0] += 1
+        copy = pltpu.make_async_remote_copy(
+            src_ref=src, dst_ref=dst, send_sem=send.at[k], recv_sem=recv.at[k],
+            device_id=partner, device_id_type=pl.DeviceIdType.MESH,
+        )
+        copy.start()
+        return copy
+
+    wmine[...] = jnp.full(wmine.shape, wts[0], f32)
+    probe_copies = [ship(probes, other, mate), ship(wmine, wother, mate)]
+
+    def reduce_rows(source, sums, got, pieces):
+        rows = psize
+        for step, (mine, partner) in enumerate(halves):
+            rows //= 2
+            away = pl.ds(pl.multiple_of((1 - mine) * rows, 8), rows)
+            copy = ship(source.at[:, away], got[step], partner)
+            yield
+            copy.wait()
+            keep = pl.ds(pl.multiple_of(mine * rows, 8), rows)
+            sums[step][...] = source[:, keep] + got[step][...]
+            source = sums[step]
+        rows //= rows_of_tiles
+        copies = []
+        for d, partner in enumerate(others):
+            away = pl.ds(pl.multiple_of(partner["ty"] * rows, 8), rows)
+            copies.append(ship(source.at[:, away], pieces.at[d], partner))
+        yield
+        for copy in copies:
+            copy.wait()
+        whole = source[:, pl.ds(pl.multiple_of(ty * rows, 8), rows)]
+        for d in range(len(others)):
+            whole = whole + pieces[d]
+        pieces[len(others)] = whole
+        yield
+
+    def spread_rows():
+        rows = psize // 2**bits // rows_of_tiles
+        first = 0
+        height = psize
+        for mine, _ in halves:
+            height //= 2
+            first = first + mine * height
+        here = pl.ds(pl.multiple_of(first + ty * rows, 8), rows)
+        whole = q_pieces[len(others)] / (e_pieces[len(others)] + damping)
+        result[:, here] = probes[0, :, here] + whole
+        copies = [ship(result.at[:, here], result.at[:, here], p) for p in others]
+        yield
+        for copy in copies:
+            copy.wait()
+        for mine, partner in reversed(halves):
+            here = pl.ds(pl.multiple_of(first, 8), height)
+            copy = ship(result.at[:, here], result.at[:, here], partner)
+            yield
+            copy.wait()
+            first = first - mine * height
+            height *= 2
+        yield
+
+    def near(f, side_probes, w):
+        pr, pi = side_probes[0, 0], side_probes[0, 1]
+        o_r, o_i = patch[f, 0], patch[f, 1]
+        real, imag = forward(pr * o_r - pi * o_i, pr * o_i + pi * o_r, right, left)
+        psi[w, f, 0] = real
+        psi[w, f, 1] = imag
+
+    def loop(low, high, body):
+        if high > low:
+            pl.loop(low, high)(body)
+
+    lighting = reduce_rows(e, e_sums, e_got, e_pieces)
+    marks = [count * i // (bits + 1) for i in range(bits + 2)]
+    for low, high in zip(marks, marks[1:]):
+        next(lighting)
+        loop(low, high, lambda f: near(f, probes, 0))
+    next(lighting)
+    for copy in probe_copies:
+        copy.wait()
+
+    w_0, w_1 = wmine[0:1, 0:1], wother[0:1, 0:1]
+    total = w_0 + w_1
+    w_0, w_1 = w_0 / total, w_1 / total
+    light[...] = (
+        probes[0, 0] * probes[0, 0] + probes[0, 1] * probes[0, 1]
+        + other[0, 0] * other[0, 0] + other[0, 1] * other[0, 1]
+    )
+
+    def both(f):
+        near(f, other, 1)
+        power = w_0 * (psi[0, f, 0] * psi[0, f, 0] + psi[0, f, 1] * psi[0, f, 1])
+        power += w_1 * (psi[1, f, 0] * psi[1, f, 0] + psi[1, f, 1] * psi[1, f, 1])
+        factor = jnp.sqrt(meas[f]) / jnp.sqrt(power + intensity_offset) - 1.0
+        for w in range(2):
+            for ch in range(2):
+                psi[w, f, ch] *= factor
+
+    loop(0, count, both)
+    q[...] = jnp.zeros_like(q)
+
+    def own(f):
+        real, imag = inverse(psi[0, f, 0], psi[0, f, 1], right, left)
+        pr, pi = probes[0, 0], probes[0, 1]
+        o_r, o_i = patch[f, 0], patch[f, 1]
+        grad[f, 0] = pr * real + pi * imag
+        grad[f, 1] = pr * imag - pi * real
+        q[0] += o_r * real + o_i * imag
+        q[1] += o_r * imag - o_i * real
+
+    loop(0, count, own)
+
+    def rest(f):
+        real, imag = inverse(psi[1, f, 0], psi[1, f, 1], right, left)
+        pr, pi = other[0, 0], other[0, 1]
+        grad[f, 0] += pr * real + pi * imag
+        grad[f, 1] += pr * imag - pi * real
+
+    gather = reduce_rows(q, q_sums, q_got, q_pieces)
+    phases = 2 * (bits + 1)
+    done = 0
+
+    def work(phase):
+        nonlocal done
+        later = 1 + (count - 1) * phase // (phases - 2) if phase else 1
+        loop(done, min(later, count), rest)
+        done = min(later, count)
+
+    for phase in range(bits + 1):
+        next(gather)
+        work(phase)
+    next(gather)
+    out = spread_rows()
+    next(out)
+    for phase in range(bits + 1, phases):
+        work(phase)
+        next(out)
+    new_probes[0] = result[...]
+
+
+def pair_step(bits, rows_of_tiles, object_field, probes, measured, positions, weights):
+    psize = probes.shape[-1]
+    side = object_field.shape[-1]
+    count = measured.shape[2]
+    right, left = tables(psize)
+    f32 = jnp.float32
+    steps = bits + rows_of_tiles - 1
+    copies = 2 + 3 * steps
+
+    def buffers(planes):
+        heights = [psize // 2 ** (b + 1) for b in range(bits)]
+        halves = [pltpu.VMEM((planes, h, psize), f32) for h in heights]
+        return halves
+
+    def pieces(planes):
+        rows = psize // 2**bits // rows_of_tiles
+        return pltpu.VMEM((rows_of_tiles, planes, rows, psize), f32)
+
+    vmem = pl.BlockSpec(memory_space=pltpu.VMEM)
+    smem = pl.BlockSpec(memory_space=pltpu.SMEM)
+    one_frame = pl.BlockSpec((1, 2, psize, psize), lambda f: (f, 0, 0, 0))
+    frames = jax.ShapeDtypeStruct((count, 2, psize, psize), f32)
+    image = jax.ShapeDtypeStruct((1, psize, psize), f32)
+    room = pltpu.CompilerParams(vmem_limit_bytes=20 * 2**20)
+    patches, e = pl.pallas_call(
+        window_kernel,
+        grid=(count,),
+        out_shape=(frames, image),
+        in_specs=[smem, vmem],
+        out_specs=(one_frame, vmem),
+        compiler_params=room,
+    )(positions[0, 0], object_field)
+    grad, light, new_probes = pl.pallas_call(
+        functools.partial(pair_kernel, bits, rows_of_tiles),
+        out_shape=(
+            frames,
+            jax.ShapeDtypeStruct((psize, psize), f32),
+            jax.ShapeDtypeStruct(probes.shape, f32),
+        ),
+        in_specs=[smem] + [vmem] * 6,
+        out_specs=(vmem,) * 3,
+        scratch_shapes=[
+            pltpu.VMEM(probes.shape, f32),
+            pltpu.VMEM((8, 128), f32),
+            pltpu.VMEM((8, 128), f32),
+            pltpu.VMEM((2, count, 2, psize, psize), f32),
+            pltpu.VMEM((2, psize, psize), f32),
+            buffers(2),
+            buffers(2),
+            buffers(1),
+            buffers(1),
+            pieces(2),
+            pieces(1),
+            pltpu.VMEM((2, psize, psize), f32),
+            pltpu.SemaphoreType.DMA((copies,)),
+            pltpu.SemaphoreType.DMA((copies,)),
+        ],
+        compiler_params=pltpu.CompilerParams(
+            vmem_limit_bytes=40 * 2**20, collective_id=0, has_side_effects=True
+        ),
+    )(weights, patches, e, probes, measured[0, 0], right, left)
+    new_object = pl.pallas_call(
+        scatter_kernel,
+        grid=(count,),
+        out_shape=jax.ShapeDtypeStruct(object_field.shape, f32),
+        in_specs=[smem, vmem, one_frame, vmem],
+        out_specs=vmem,
+        scratch_shapes=[pltpu.VMEM((side, side), f32)],
+        compiler_params=room,
+    )(positions[0, 0], object_field, grad, light)
+    return (new_object, new_probes)
+
+
 def solution(mesh):
     in_specs = (
         P(None, "ty", "tx"),
@@ -193,5 +489,10 @@
         P("wave"),
     )
     out_specs = (P(None, "ty", "tx"), P("wave", None, None, None))
-    body = functools.partial(local, mesh.shape["wave"])
+    waves, rows_of_tiles, tiles = (mesh.shape[axis] for axis in ("wave", "ty", "tx"))
+    bits = tiles.bit_length() - 1
+    if waves == 2 and rows_of_tiles > 1 and bits >= 1 and 2**bits == tiles:
+        body = functools.partial(pair_step, bits, rows_of_tiles)
+    else:
+        body = functools.partial(local, waves)
     return jax.shard_map(body, mesh=mesh, in_specs=in_specs, out_specs=out_specs, check_vma=False)

time: 175 us -> 79.5 us (0.45)
  waiting for transfers between devices: 105 us -> 0 us
  Pallas kernels: 44.7 us -> 71.1 us
  between operations: 14.7 us -> 1.32 us
  other arithmetic: 6.29 us -> 0 us
  local copies, waits for them, and re-layouts: 1.35 us -> 6.72 us
  starting transfers between devices: 3.18 us -> 0 us
    psum x1 -> x0, waiting for transfers between devices: 94.5 us -> none  [local(): q, e = lax.psum((q, e), ('ty', 'tx'))]
    pallas_call x1 -> x3, Pallas kernels: 44.7 us -> 71.1 us  [the longest x1 59.2 us: pair_step(): pl.pallas_call(functools.partial(pair_kernel, bits, rows_of_tiles), out_s...]
    ppermute x2 -> x0, waiting for transfers between devices: 10.1 us -> none  [the longest x1 10.1 us: local(): all_weights.append(lax.ppermute(weights, 'wave', ring))]
    unnamed x2 -> x13, local copies, waits for them, and re-layouts: 0.01 us -> 5.97 us
    concatenate x2 -> x0, other arithmetic: 3.4 us -> none  [the longest x1 2.11 us: local(): all_probes = jnp.concatenate(all_probes)]
    ppermute x2 -> x0, starting transfers between devices: 3.14 us -> none  [the longest x1 3.06 us: local(): all_probes.append(lax.ppermute(probes, 'wave', ring))]
    add x2 -> x0, other arithmetic: 2.89 us -> none  [local(): new_probes = probes + (q / (e + damping))[None]]
  transfers between devices with their start and end apart: 3 -> 0, of which waited for: 2 -> 0; matrix products, arithmetic and copies ran while one was open for 2% -> 0% of each run, Pallas kernels for 0% -> 0%
where the time goes in v1:
time: 79.5 us; the launch traced here: 79.2 us
  Pallas kernels  71.1 us (89%)
  local copies, waits for them, and re-layouts  6.72 us (8%)
  between operations  1.32 us (2%)
    pallas_call x1, Pallas kernels, pair_step(): pl.pallas_call(functools.partial(pair_kernel, bits, rows_of_tiles), out_s...  59.2 us
    pallas_call x1, Pallas kernels, pair_step(): pl.pallas_call(scatter_kernel, grid=(count,), out_shape=jax.ShapeDtypeStr...  6.77 us
    unnamed x13, local copies, waits for them, and re-layouts  5.97 us
    pallas_call x1, Pallas kernels, pair_step(): pl.pallas_call(window_kernel, grid=(count,), out_shape=(frames, image), i...  5.14 us

profile of v1, /device:TPU:0, one launch (start us, length us, event | category | flops | bytes accessed | tf_op | source)
XLA Modules:
  0.0 79.2 jit_solution(11342787889704334329)
XLA Ops:
  1.3 0.8 copy.10.pos
  2.0 0.0 copy-start
  2.0 1.6 %copy-done = f32[2,512,512]{2,1,0:T(8,128)S(1)} copy-done((f32[2,512,512]{2,1,0:T(8,128)S(1)}, f32[2,512,512]{2,1,0:T(8,128)}, u32[]{:S(2)}) %copy-start) | copy-done | bytes 2097176
  3.6 0.0 copy-start.2
  3.6 5.1 %shard_map.86 = (f32[8,2,256,256]{3,2,1,0:T(8,128)S(1)}, f32[1,256,256]{2,1,0:T(8,128)S(1)}) custom-call(s32[8,2]{1,0:T(8,128)S(1)} %copy.10.pos, f32[2,512,512]{2,1,0:T(8,128)S(1)} %copy-done), custom_call_target="tpu_custom_call" | custom-call | tf_op jit(solution)/shard_map/pallas_call | solution.py:434
  8.8 0.0 copy-done.2
  8.8 0.0 copy-start.3
  8.8 1.3 %copy-done.3 = bf16[3,256,768]{2,1,0:T(8,128)(2,1)S(1)} copy-done((bf16[3,256,768]{2,1,0:T(8,128)(2,1)S(1)}, bf16[3,256,768]{2,1,0:T(8,128)(2,1)}, u32[]{:S(2)}) %copy-start.3) | copy-done | bytes 1179672
  10.1 0.0 copy-start.4
  10.1 1.3 %copy-done.4 = bf16[3,768,256]{2,1,0:T(8,128)(2,1)S(1)} copy-done((bf16[3,768,256]{2,1,0:T(8,128)(2,1)S(1)}, bf16[3,768,256]{2,1,0:T(8,128)(2,1)}, u32[]{:S(2)}) %copy-start.4) | copy-done | bytes 1179672
  11.3 0.0 copy-start.5
  11.3 1.0 %copy-done.5 = f32[1,2,256,256]{3,2,1,0:T(8,128)S(1)} copy-done((f32[1,2,256,256]{3,2,1,0:T(8,128)S(1)}, f32[1,2,256,256]{3,2,1,0:T(8,128)}, u32[]{:S(2)}) %copy-start.5) | copy-done | bytes 524312
  12.4 0.0 copy-start.1
  12.4 59.2 %shard_map.87 = (f32[8,2,256,256]{3,2,1,0:T(8,128)S(1)}, f32[256,256]{1,0:T(8,128)S(1)}, f32[1,2,256,256]{3,2,1,0:T(8,128)S(1)}) custom-call(f32[1]{0:T(128)S(6)} %copy.12.wts, f32[8,2,256,256]{3,2,1,0:T(8,128)S(1)} %get-tuple-element.7.patch, f32[1,256,256]{2,1,0:T(8,128)S(1)} %get-tuple-element.8.e, f32[1,2,256,256]{3,2,1,0:T(8,128)S(1)} %copy-done.5, ...), custom_call_target="tpu_custom_call" | custom-call | tf_op jit(solution)/shard_map/pallas_call | solution.py:442
  71.6 0.0 copy-done.1
  71.6 6.8 %shard_map.88 = f32[2,512,512]{2,1,0:T(8,128)} custom-call(s32[8,2]{1,0:T(8,128)S(1)} %copy.10.pos, f32[2,512,512]{2,1,0:T(8,128)S(1)} %copy-done.1, f32[8,2,256,256]{3,2,1,0:T(8,128)S(1)} %get-tuple-element.9.grad, f32[256,256]{1,0:T(8,128)S(1)} %get-tuple-element.10.light), custom_call_target="tpu_custom_call" | custom-call | tf_op jit(solution)/shard_map/pallas_call | solution.py:471
  78.4 0.8 %copy.13 = f32[1,2,256,256]{3,2,1,0:T(8,128)} copy(f32[1,2,256,256]{3,2,1,0:T(8,128)S(1)} %get-tuple-element.15) | data formatting | bytes 1048576
Async XLA Ops:
  2.0 1.6 %copy-start = (f32[2,512,512]{2,1,0:T(8,128)S(1)}, f32[2,512,512]{2,1,0:T(8,128)}, u32[]{:S(2)}) copy-start(f32[2,512,512]{2,1,0:T(8,128)} %obj.3) | copy-start | bytes 6291460
  3.6 5.2 %copy-start.2 = (f32[1,1,8,256,256]{4,3,2,1,0:T(8,128)S(1)}, f32[1,1,8,256,256]{4,3,2,1,0:T(8,128)}, u32[]{:S(2)}) copy-start(f32[1,1,8,256,256]{4,3,2,1,0:T(8,128)} %param.9) | copy-start | bytes 6291460
  8.8 1.3 %copy-start.3 = (bf16[3,256,768]{2,1,0:T(8,128)(2,1)S(1)}, bf16[3,256,768]{2,1,0:T(8,128)(2,1)}, u32[]{:S(2)}) copy-start(bf16[3,256,768]{2,1,0:T(8,128)(2,1)} %constant.5.clone.left) | copy-start | bytes 3538948
  10.1 1.3 %copy-start.4 = (bf16[3,768,256]{2,1,0:T(8,128)(2,1)S(1)}, bf16[3,768,256]{2,1,0:T(8,128)(2,1)}, u32[]{:S(2)}) copy-start(bf16[3,768,256]{2,1,0:T(8,128)(2,1)} %constant.4.clone.right) | copy-start | bytes 3538948
  11.3 1.0 %copy-start.5 = (f32[1,2,256,256]{3,2,1,0:T(8,128)S(1)}, f32[1,2,256,256]{3,2,1,0:T(8,128)}, u32[]{:S(2)}) copy-start(f32[1,2,256,256]{3,2,1,0:T(8,128)} %probes.1) | copy-start | bytes 1572868
  12.4 59.2 %copy-start.1 = (f32[2,512,512]{2,1,0:T(8,128)S(1)}, f32[2,512,512]{2,1,0:T(8,128)}, u32[]{:S(2)}) copy-start(f32[2,512,512]{2,1,0:T(8,128)} %obj.3) | copy-start | bytes 6291460

commit v2 on v1

--- a/solution.py
+++ b/solution.py
@@ -18,13 +18,19 @@
     angles = 2.0 * math.pi / length * (indices[:, None] * indices[None, :] % length)
     cosine = np.cos(angles) / math.sqrt(length)
     sine = -np.sin(angles) / math.sqrt(length)
-    right = []
-    for table in (cosine, sine - cosine, sine + cosine):
+    half = length // 2
+    parts = []
+    for odd in range(2):
+        c, s = cosine[:half, odd::2], sine[:half, odd::2]
+        parts.append(np.block([[c, s], [-s, c]]))
+    both = []
+    for table in parts + [part.T for part in parts]:
         high = table.astype(jnp.bfloat16)
         low = (table - high.astype(np.float64)).astype(jnp.bfloat16)
-        right.append(np.concatenate([high, high, low], axis=0))
-    right = np.stack(right)
-    return right, np.ascontiguousarray(right.transpose(0, 2, 1))
+        both.append(np.stack([high, low]))
+    order = np.concatenate([indices[0::2], indices[1::2]])
+    shuffle = (indices[:, None] == order[None, :]).astype(jnp.bfloat16)
+    return np.stack(both), np.stack([shuffle, shuffle.T])
 
 
 def split(x):
@@ -33,36 +39,55 @@
     return high, low
 
 
-def times_right(x, table):
+def times(x, table, which, axis):
     high, low = split(x)
-    return jnp.dot(
-        jnp.concatenate([high, low, high], axis=1), table, preferred_element_type=jnp.float32
-    )
-
-
-def times_left(x, table):
-    high, low = split(x)
-    return jnp.dot(
-        table, jnp.concatenate([high, low, high], axis=0), preferred_element_type=jnp.float32
-    )
-
-
-def forward(real, imag, right, left):
-    for times, table in ((times_right, right), (times_left, left)):
-        both = times(real + imag, table[0])
-        real, imag = both - times(imag, table[2]), both + times(real, table[1])
+    x = jnp.concatenate([high, low, high], axis=axis)
+    which = which if axis == 1 else (which + 2) % 4
+    high, low = table[which, 0], table[which, 1]
+    table = jnp.concatenate([high, high, low], axis=1 - axis)
+    pair = (x, table) if axis == 1 else (table, x)
+    return jnp.dot(*pair, preferred_element_type=jnp.float32)
+
+
+def halves_of(x, axis):
+    half = x.shape[axis] // 2
+    return (x[:, :half], x[:, half:]) if axis == 1 else (x[:half], x[half:])
+
+
+def forward(real, imag, table):
+    for axis in (1, 0):
+        (r0, r1), (i0, i1) = halves_of(real, axis), halves_of(imag, axis)
+        even = times(jnp.concatenate([r0 + r1, i0 + i1], axis), table, 0, axis)
+        odd = times(jnp.concatenate([r0 - r1, i0 - i1], axis), table, 1, axis)
+        (er, ei), (o_r, oi) = halves_of(even, axis), halves_of(odd, axis)
+        real = jnp.concatenate([er, o_r], axis)
+        imag = jnp.concatenate([ei, oi], axis)
     return real, imag
 
 
-def inverse(real, imag, right, left):
-    for times, table in ((times_right, right), (times_left, left)):
-        both = times(real + imag, table[0])
-        real, imag = both + times(imag, table[1]), both - times(real, table[2])
+def inverse(real, imag, table):
+    for axis in (1, 0):
+        (er, o_r), (ei, oi) = halves_of(real, axis), halves_of(imag, axis)
+        even = times(jnp.concatenate([er, ei], axis), table, 2, axis)
+        odd = times(jnp.concatenate([o_r, oi], axis), table, 3, axis)
+        (r0, i0), (r1, i1) = halves_of(even + odd, axis), halves_of(even - odd, axis)
+        real = jnp.concatenate([r0, r1], axis)
+        imag = jnp.concatenate([i0, i1], axis)
     return real, imag
 
 
+def amplitude(meas, f, order):
+    root = jnp.sqrt(meas[f])
+    for axis in (1, 0):
+        both = jnp.concatenate(split(root), axis)
+        twice = jnp.concatenate([order[1 - axis]] * 2, 1 - axis)
+        pair = (both, twice) if axis == 1 else (twice, both)
+        root = jnp.dot(*pair, preferred_element_type=jnp.float32)
+    return root
+
+
 def step_kernel(
-    pos, wts, obj, probes, meas, right, left, new_obj, q, e, patch, psi, hacc, light, grad, power
+    pos, wts, obj, probes, meas, table, order, new_obj, q, e, patch, psi, hacc, light, grad, power
 ):
     waves = probes.shape[0]
     count = meas.shape[0]
@@ -106,20 +131,21 @@
         def far(w):
             pr, pi = probes[w, 0], probes[w, 1]
             o_r, o_i = patch[0], patch[1]
-            real, imag = forward(pr * o_r - pi * o_i, pr * o_i + pi * o_r, right, left)
+            real, imag = forward(pr * o_r - pi * o_i, pr * o_i + pi * o_r, table)
             psi[w, 0] = real
             psi[w, 1] = imag
             power[...] += wts[w] * (real * real + imag * imag)
 
         each_wave(0, far)
         power[...] = (
-            jnp.sqrt(meas[f]) / jnp.sqrt(power[...] * inv_total + intensity_offset) - 1.0
+            amplitude(meas, f, order) / jnp.sqrt(power[...] * inv_total + intensity_offset)
+            - 1.0
         )
         grad[...] = jnp.zeros_like(grad)
 
         def near(w):
             factor = power[...]
-            real, imag = inverse(psi[w, 0] * factor, psi[w, 1] * factor, right, left)
+            real, imag = inverse(psi[w, 0] * factor, psi[w, 1] * factor, table)
             pr, pi = probes[w, 0], probes[w, 1]
             grad[0] += pr * real + pi * imag
             grad[1] += pr * imag - pi * real
@@ -149,7 +175,7 @@
 def local(waves, object_field, probes, measured, positions, weights):
     psize = probes.shape[-1]
     side = object_field.shape[-1]
-    right, left = tables(psize)
+    table, order = tables(psize)
     all_probes, all_weights = [probes], [weights]
     for turn in range(1, waves):
         ring = [(i, (i + turn) % waves) for i in range(waves)]
@@ -178,7 +204,7 @@
             pltpu.VMEM((psize, psize), f32),
         ],
         compiler_params=pltpu.CompilerParams(vmem_limit_bytes=60 * 2**20),
-    )(positions[0, 0], all_weights, object_field, all_probes, measured[0, 0], right, left)
+    )(positions[0, 0], all_weights, object_field, all_probes, measured[0, 0], table, order)
     q, e = lax.psum((q, e), ("ty", "tx"))
     new_probes = probes + (q / (e + damping))[None]
     return (new_object, new_probes)
@@ -241,7 +267,7 @@
 
 def pair_kernel(
     bits, rows_of_tiles,
-    wts, patch, e, probes, meas, right, left,
+    wts, patch, e, probes, meas, table, order,
     grad, light, new_probes,
     other, wmine, wother, psi, q, q_sums, q_got, e_sums, e_got, q_pieces, e_pieces, result,
     send, recv,
@@ -331,7 +357,7 @@
     def near(f, side_probes, w):
         pr, pi = side_probes[0, 0], side_probes[0, 1]
         o_r, o_i = patch[f, 0], patch[f, 1]
-        real, imag = forward(pr * o_r - pi * o_i, pr * o_i + pi * o_r, right, left)
+        real, imag = forward(pr * o_r - pi * o_i, pr * o_i + pi * o_r, table)
         psi[w, f, 0] = real
         psi[w, f, 1] = imag
 
@@ -360,7 +386,7 @@
         near(f, other, 1)
         power = w_0 * (psi[0, f, 0] * psi[0, f, 0] + psi[0, f, 1] * psi[0, f, 1])
         power += w_1 * (psi[1, f, 0] * psi[1, f, 0] + psi[1, f, 1] * psi[1, f, 1])
-        factor = jnp.sqrt(meas[f]) / jnp.sqrt(power + intensity_offset) - 1.0
+        factor = amplitude(meas, f, order) / jnp.sqrt(power + intensity_offset) - 1.0
         for w in range(2):
             for ch in range(2):
                 psi[w, f, ch] *= factor
@@ -369,7 +395,7 @@
     q[...] = jnp.zeros_like(q)
 
     def own(f):
-        real, imag = inverse(psi[0, f, 0], psi[0, f, 1], right, left)
+        real, imag = inverse(psi[0, f, 0], psi[0, f, 1], table)
         pr, pi = probes[0, 0], probes[0, 1]
         o_r, o_i = patch[f, 0], patch[f, 1]
         grad[f, 0] = pr * real + pi * imag
@@ -380,7 +406,7 @@
     loop(0, count, own)
 
     def rest(f):
-        real, imag = inverse(psi[1, f, 0], psi[1, f, 1], right, left)
+        real, imag = inverse(psi[1, f, 0], psi[1, f, 1], table)
         pr, pi = other[0, 0], other[0, 1]
         grad[f, 0] += pr * real + pi * imag
         grad[f, 1] += pr * imag - pi * real
@@ -411,7 +437,7 @@
     psize = probes.shape[-1]
     side = object_field.shape[-1]
     count = measured.shape[2]
-    right, left = tables(psize)
+    table, order = tables(psize)
     f32 = jnp.float32
     steps = bits + rows_of_tiles - 1
     copies = 2 + 3 * steps
@@ -430,7 +456,7 @@
     one_frame = pl.BlockSpec((1, 2, psize, psize), lambda f: (f, 0, 0, 0))
     frames = jax.ShapeDtypeStruct((count, 2, psize, psize), f32)
     image = jax.ShapeDtypeStruct((1, psize, psize), f32)
-    room = pltpu.CompilerParams(vmem_limit_bytes=20 * 2**20)
+    room = pltpu.CompilerParams(vmem_limit_bytes=60 * 2**20)
     patches, e = pl.pallas_call(
         window_kernel,
         grid=(count,),
@@ -465,9 +491,9 @@
             pltpu.SemaphoreType.DMA((copies,)),
         ],
         compiler_params=pltpu.CompilerParams(
-            vmem_limit_bytes=40 * 2**20, collective_id=0, has_side_effects=True
+            vmem_limit_bytes=60 * 2**20, collective_id=0, has_side_effects=True
         ),
-    )(weights, patches, e, probes, measured[0, 0], right, left)
+    )(weights, patches, e, probes, measured[0, 0], table, order)
     new_object = pl.pallas_call(
         scatter_kernel,
         grid=(count,),

time: 79.5 us -> 82.4 us (1.036)
  Pallas kernels: 71.1 us -> 78.7 us
  local copies, waits for them, and re-layouts: 6.72 us -> 2.15 us
    unnamed x13 -> x3, local copies, waits for them, and re-layouts: 5.97 us -> 0.8 us
    pallas_call x1, Pallas kernels: 6.77 us -> 9.62 us  [pair_step(): pl.pallas_call(scatter_kernel, grid=(count,), out_shape=jax.ShapeDtypeStr...]
    pallas_call x1, Pallas kernels: 5.14 us -> 7.62 us  [pair_step(): pl.pallas_call(window_kernel, grid=(count,), out_shape=(frames, image), i...]
    pallas_call x1, Pallas kernels: 59.2 us -> 61.4 us  [pair_step(): pl.pallas_call(functools.partial(pair_kernel, bits, rows_of_tiles), out_s...]
where the time goes in v2:
time: 82.4 us; the launch traced here: 82.1 us
  Pallas kernels  78.7 us (96%)
  local copies, waits for them, and re-layouts  2.15 us (3%)
  between operations  1.29 us (2%)
    pallas_call x1, Pallas kernels, pair_step(): pl.pallas_call(functools.partial(pair_kernel, bits, rows_of_tiles), out_s...  61.4 us
    pallas_call x1, Pallas kernels, pair_step(): pl.pallas_call(scatter_kernel, grid=(count,), out_shape=jax.ShapeDtypeStr...  9.62 us
    pallas_call x1, Pallas kernels, pair_step(): pl.pallas_call(window_kernel, grid=(count,), out_shape=(frames, image), i...  7.62 us

profile of v2, /device:TPU:0, one launch (start us, length us, event | category | flops | bytes accessed | tf_op | source)
XLA Modules:
  0.0 82.1 jit_solution(17921509821744374963)
XLA Ops:
  1.3 1.3 %copy.10.pos = s32[8,2]{1,0:T(8,128)} copy(s32[8,2]{0,1:T(2,128)} %bitcast.3) | data formatting | bytes 128 | tf_op jit(solution)/shard_map/squeeze | solution.py:505
  2.6 7.6 %shard_map.86 = (f32[8,2,256,256]{3,2,1,0:T(8,128)}, f32[1,256,256]{2,1,0:T(8,128)}) custom-call(s32[8,2]{1,0:T(8,128)} %copy.10.pos, f32[2,512,512]{2,1,0:T(8,128)} %obj.3), custom_call_target="tpu_custom_call" | custom-call | tf_op jit(solution)/shard_map/pallas_call | solution.py:460
  10.2 61.4 %shard_map.87 = (f32[8,2,256,256]{3,2,1,0:T(8,128)}, f32[256,256]{1,0:T(8,128)}, f32[1,2,256,256]{3,2,1,0:T(8,128)}) custom-call(f32[1]{0:T(128)S(6)} %copy.12.wts, f32[8,2,256,256]{3,2,1,0:T(8,128)} %get-tuple-element.7.patch, f32[1,256,256]{2,1,0:T(8,128)} %get-tuple-element.8.e, f32[1,2,256,256]{3,2,1,0:T(8,128)} %probes.1, f32[8,256,256]{2,1,0:T(8,128)} %bitcast.2, ...), custom_call_target="tpu_custom_call" | custom-call | tf_op jit(solution)/shard_map/pallas_call | solution.py:468
  71.7 0.0 copy-start
  71.7 9.6 %shard_map.88 = f32[2,512,512]{2,1,0:T(8,128)} custom-call(s32[8,2]{1,0:T(8,128)} %copy.10.pos, f32[2,512,512]{2,1,0:T(8,128)} %obj.3, f32[8,2,256,256]{3,2,1,0:T(8,128)} %get-tuple-element.9.grad, f32[256,256]{1,0:T(8,128)} %get-tuple-element.10.light), custom_call_target="tpu_custom_call" | custom-call | tf_op jit(solution)/shard_map/pallas_call | solution.py:497
  81.3 0.0 copy-done
  81.3 0.8 copy.13
Async XLA Ops:
  71.7 9.6 %copy-start = (f32[1,2,256,256]{3,2,1,0:T(8,128)S(1)}, f32[1,2,256,256]{3,2,1,0:T(8,128)}, u32[]{:S(2)}) copy-start(f32[1,2,256,256]{3,2,1,0:T(8,128)} %get-tuple-element.15) | copy-start | bytes 1572868

commit v3 on v2

--- a/solution.py
+++ b/solution.py
@@ -216,6 +216,24 @@
     return base, r - base, c
 
 
+def raise_rows(rows, shift):
+    rows = rows.reshape(-1, 8, rows.shape[-1])
+    rows = pltpu.roll(rows, lax.rem(8 - shift, 8), 1)
+    within = lax.broadcasted_iota(jnp.int32, rows[1:].shape, 1)
+    rows = jnp.where(within < 8 - shift, rows[:-1], rows[1:])
+    return rows.reshape(-1, rows.shape[-1])
+
+
+def lower_rows(rows, shift):
+    rows = rows.reshape(-1, 8, rows.shape[-1])
+    rows = pltpu.roll(rows, lax.rem(shift, 8), 1)
+    none = jnp.zeros((1,) + rows.shape[1:], rows.dtype)
+    below, above = jnp.concatenate([rows, none], 0), jnp.concatenate([none, rows], 0)
+    within = lax.broadcasted_iota(jnp.int32, below.shape, 1)
+    rows = jnp.where(within >= shift, below, above)
+    return rows.reshape(-1, rows.shape[-1])
+
+
 def window_kernel(pos, obj, patch, e):
     psize, side = patch.shape[-1], obj.shape[-1]
     tall = psize + 8
@@ -224,7 +242,7 @@
     power = jnp.zeros((psize, psize), jnp.float32)
     for ch in range(2):
         rows = pltpu.roll(obj[ch, pl.ds(base, tall), :], lax.rem(side - c, side), 1)[:, :psize]
-        rows = pltpu.roll(rows, lax.rem(tall - shift, tall), 0)[:psize]
+        rows = raise_rows(rows, shift)
         patch[0, ch] = rows
         power += rows * rows
 
@@ -249,8 +267,7 @@
         hacc[...] = jnp.zeros_like(hacc)
 
     def place(window):
-        below = jnp.zeros((tall - psize, psize), jnp.float32)
-        window = pltpu.roll(jnp.concatenate([window, below], 0), shift, 0)
+        window = lower_rows(window, shift)
         beside = jnp.zeros((tall, side - psize), jnp.float32)
         return pltpu.roll(jnp.concatenate([window, beside], 1), c, 1)
 
@@ -304,7 +321,12 @@
         return copy
 
     wmine[...] = jnp.full(wmine.shape, wts[0], f32)
-    probe_copies = [ship(probes, other, mate), ship(wmine, wother, mate)]
+    core, twin = halves[0]
+    strip = pl.ds(pl.multiple_of(core * (psize // 2), 8), psize // 2)
+    probe_copies = [
+        ship(probes.at[:, :, strip], other.at[:, :, strip], mate),
+        ship(wmine, wother, mate),
+    ]
 
     def reduce_rows(source, sums, got, pieces):
         rows = psize
@@ -366,13 +388,13 @@
             pl.loop(low, high)(body)
 
     lighting = reduce_rows(e, e_sums, e_got, e_pieces)
-    marks = [count * i // (bits + 1) for i in range(bits + 2)]
-    for low, high in zip(marks, marks[1:]):
-        next(lighting)
-        loop(low, high, lambda f: near(f, probes, 0))
     next(lighting)
+    loop(0, count, lambda f: near(f, probes, 0))
     for copy in probe_copies:
         copy.wait()
+    copy = ship(other.at[:, :, strip], other.at[:, :, strip], twin)
+    next(lighting)
+    copy.wait()
 
     w_0, w_1 = wmine[0:1, 0:1], wother[0:1, 0:1]
     total = w_0 + w_1
@@ -391,7 +413,10 @@
             for ch in range(2):
                 psi[w, f, ch] *= factor
 
-    loop(0, count, both)
+    marks = [count * i // bits for i in range(bits + 1)]
+    for low, high in zip(marks, marks[1:]):
+        loop(low, high, both)
+        next(lighting)
     q[...] = jnp.zeros_like(q)
 
     def own(f):
@@ -440,7 +465,7 @@
     table, order = tables(psize)
     f32 = jnp.float32
     steps = bits + rows_of_tiles - 1
-    copies = 2 + 3 * steps
+    copies = 3 + 3 * steps
 
     def buffers(planes):
         heights = [psize // 2 ** (b + 1) for b in range(bits)]

time: 82.4 us -> 77.2 us (0.937)
  Pallas kernels: 78.7 us -> 73.5 us
    pallas_call x1, Pallas kernels: 61.4 us -> 57.2 us  [pair_step(): pl.pallas_call(functools.partial(pair_kernel, bits, rows_of_tiles), out_s...]
where the time goes in v3:
time: 77.2 us; the launch traced here: 76.9 us
  Pallas kernels  73.5 us (95%)
  local copies, waits for them, and re-layouts  2.15 us (3%)
  between operations  1.29 us (2%)
    pallas_call x1, Pallas kernels, pair_step(): pl.pallas_call(functools.partial(pair_kernel, bits, rows_of_tiles), out_s...  57.2 us
    pallas_call x1, Pallas kernels, pair_step(): pl.pallas_call(scatter_kernel, grid=(count,), out_shape=jax.ShapeDtypeStr...  9.22 us
    pallas_call x1, Pallas kernels, pair_step(): pl.pallas_call(window_kernel, grid=(count,), out_shape=(frames, image), i...  7.11 us

profile of v3, /device:TPU:0, one launch (start us, length us, event | category | flops | bytes accessed | tf_op | source)
XLA Modules:
  0.0 76.9 jit_solution(12337736618729951511)
XLA Ops:
  1.3 1.3 %copy.10.pos = s32[8,2]{1,0:T(8,128)} copy(s32[8,2]{0,1:T(2,128)} %bitcast.3) | data formatting | bytes 128 | tf_op jit(solution)/shard_map/squeeze | solution.py:530
  2.6 7.1 %shard_map.86 = (f32[8,2,256,256]{3,2,1,0:T(8,128)}, f32[1,256,256]{2,1,0:T(8,128)}) custom-call(s32[8,2]{1,0:T(8,128)} %copy.10.pos, f32[2,512,512]{2,1,0:T(8,128)} %obj.3), custom_call_target="tpu_custom_call" | custom-call | tf_op jit(solution)/shard_map/pallas_call | solution.py:485
  9.7 57.2 %shard_map.87 = (f32[8,2,256,256]{3,2,1,0:T(8,128)}, f32[256,256]{1,0:T(8,128)}, f32[1,2,256,256]{3,2,1,0:T(8,128)}) custom-call(f32[1]{0:T(128)S(6)} %copy.12.wts, f32[8,2,256,256]{3,2,1,0:T(8,128)} %get-tuple-element.7.patch, f32[1,256,256]{2,1,0:T(8,128)} %get-tuple-element.8.e, f32[1,2,256,256]{3,2,1,0:T(8,128)} %probes.1, f32[8,256,256]{2,1,0:T(8,128)} %bitcast.2, ...), custom_call_target="tpu_custom_call" | custom-call | tf_op jit(solution)/shard_map/pallas_call | solution.py:493
  66.9 0.0 copy-start
  66.9 9.2 %shard_map.88 = f32[2,512,512]{2,1,0:T(8,128)} custom-call(s32[8,2]{1,0:T(8,128)} %copy.10.pos, f32[2,512,512]{2,1,0:T(8,128)} %obj.3, f32[8,2,256,256]{3,2,1,0:T(8,128)} %get-tuple-element.9.grad, f32[256,256]{1,0:T(8,128)} %get-tuple-element.10.light), custom_call_target="tpu_custom_call" | custom-call | tf_op jit(solution)/shard_map/pallas_call | solution.py:522
  76.1 0.0 copy-done
  76.1 0.8 %copy.13 = f32[1,2,256,256]{3,2,1,0:T(8,128)} copy(f32[1,2,256,256]{3,2,1,0:T(8,128)S(1)} %copy-done) | data formatting | bytes 1048576
Async XLA Ops:
  66.9 9.2 %copy-start = (f32[1,2,256,256]{3,2,1,0:T(8,128)S(1)}, f32[1,2,256,256]{3,2,1,0:T(8,128)}, u32[]{:S(2)}) copy-start(f32[1,2,256,256]{3,2,1,0:T(8,128)} %get-tuple-element.15) | copy-start | bytes 1572868

commit v4 on v3

--- a/solution.py
+++ b/solution.py
@@ -481,7 +481,7 @@
     one_frame = pl.BlockSpec((1, 2, psize, psize), lambda f: (f, 0, 0, 0))
     frames = jax.ShapeDtypeStruct((count, 2, psize, psize), f32)
     image = jax.ShapeDtypeStruct((1, psize, psize), f32)
-    room = pltpu.CompilerParams(vmem_limit_bytes=60 * 2**20)
+    room = pltpu.CompilerParams(vmem_limit_bytes=20 * 2**20)
     patches, e = pl.pallas_call(
         window_kernel,
         grid=(count,),
@@ -516,7 +516,7 @@
             pltpu.SemaphoreType.DMA((copies,)),
         ],
         compiler_params=pltpu.CompilerParams(
-            vmem_limit_bytes=60 * 2**20, collective_id=0, has_side_effects=True
+            vmem_limit_bytes=40 * 2**20, collective_id=0, has_side_effects=True
         ),
     )(weights, patches, e, probes, measured[0, 0], table, order)
     new_object = pl.pallas_call(

time: 77.2 us -> 69.4 us (0.90)
  Pallas kernels: 73.5 us -> 61.4 us
  local copies, waits for them, and re-layouts: 2.15 us -> 6.36 us
    pallas_call x1, Pallas kernels: 57.2 us -> 51 us  [pair_step(): pl.pallas_call(functools.partial(pair_kernel, bits, rows_of_tiles), out_s...]
    unnamed x3 -> x13, local copies, waits for them, and re-layouts: 0.8 us -> 5.6 us
    pallas_call x1, Pallas kernels: 9.22 us -> 6.13 us  [pair_step(): pl.pallas_call(scatter_kernel, grid=(count,), out_shape=jax.ShapeDtypeStr...]
    pallas_call x1, Pallas kernels: 7.11 us -> 4.23 us  [pair_step(): pl.pallas_call(window_kernel, grid=(count,), out_shape=(frames, image), i...]
where the time goes in v4:
time: 69.4 us; the launch traced here: 69.1 us
  Pallas kernels  61.4 us (88%)
  local copies, waits for them, and re-layouts  6.36 us (9%)
  between operations  1.32 us (2%)
    pallas_call x1, Pallas kernels, pair_step(): pl.pallas_call(functools.partial(pair_kernel, bits, rows_of_tiles), out_s...  51 us
    pallas_call x1, Pallas kernels, pair_step(): pl.pallas_call(scatter_kernel, grid=(count,), out_shape=jax.ShapeDtypeStr...  6.13 us
    unnamed x13, local copies, waits for them, and re-layouts  5.6 us
    pallas_call x1, Pallas kernels, pair_step(): pl.pallas_call(window_kernel, grid=(count,), out_shape=(frames, image), i...  4.23 us

profile of v4, /device:TPU:0, one launch (start us, length us, event | category | flops | bytes accessed | tf_op | source)
XLA Modules:
  0.0 69.1 jit_solution(6816518546393236254)
XLA Ops:
  1.3 0.8 %copy.10.pos = s32[8,2]{1,0:T(8,128)S(1)} copy(s32[8,2]{0,1:T(2,128)} %bitcast.3) | data formatting | bytes 128 | tf_op jit(solution)/shard_map/squeeze | solution.py:530
  2.0 0.0 copy-start
  2.0 1.6 %copy-done = f32[2,512,512]{2,1,0:T(8,128)S(1)} copy-done((f32[2,512,512]{2,1,0:T(8,128)S(1)}, f32[2,512,512]{2,1,0:T(8,128)}, u32[]{:S(2)}) %copy-start) | copy-done | bytes 2097176
  3.6 0.0 copy-start.2
  3.6 4.2 %shard_map.86 = (f32[8,2,256,256]{3,2,1,0:T(8,128)S(1)}, f32[1,256,256]{2,1,0:T(8,128)S(1)}) custom-call(s32[8,2]{1,0:T(8,128)S(1)} %copy.10.pos, f32[2,512,512]{2,1,0:T(8,128)S(1)} %copy-done), custom_call_target="tpu_custom_call" | custom-call | tf_op jit(solution)/shard_map/pallas_call | solution.py:485
  7.9 0.0 copy-done.2
  7.9 0.0 copy-start.3
  7.9 1.2 %copy-done.3 = bf16[4,2,256,256]{3,2,1,0:T(8,128)(2,1)S(1)} copy-done((bf16[4,2,256,256]{3,2,1,0:T(8,128)(2,1)S(1)}, bf16[4,2,256,256]{3,2,1,0:T(8,128)(2,1)}, u32[]{:S(2)}) %copy-start.3) | copy-done | bytes 1048600
  9.1 0.0 copy-start.4
  9.1 1.0 %copy-done.4 = f32[1,2,256,256]{3,2,1,0:T(8,128)S(1)} copy-done((f32[1,2,256,256]{3,2,1,0:T(8,128)S(1)}, f32[1,2,256,256]{3,2,1,0:T(8,128)}, u32[]{:S(2)}) %copy-start.4) | copy-done | bytes 524312
  10.1 0.0 copy-start.5
  10.1 0.9 %copy-done.5 = bf16[2,256,256]{2,1,0:T(8,128)(2,1)S(1)} copy-done((bf16[2,256,256]{2,1,0:T(8,128)(2,1)S(1)}, bf16[2,256,256]{2,1,0:T(8,128)(2,1)}, u32[]{:S(2)}) %copy-start.5) | copy-done | bytes 262168
  11.1 0.0 copy-start.1
  11.1 51.0 %shard_map.87 = (f32[8,2,256,256]{3,2,1,0:T(8,128)S(1)}, f32[256,256]{1,0:T(8,128)S(1)}, f32[1,2,256,256]{3,2,1,0:T(8,128)S(1)}) custom-call(f32[1]{0:T(128)S(6)} %copy.12.wts, f32[8,2,256,256]{3,2,1,0:T(8,128)S(1)} %get-tuple-element.7.patch, f32[1,256,256]{2,1,0:T(8,128)S(1)} %get-tuple-element.8.e, f32[1,2,256,256]{3,2,1,0:T(8,128)S(1)} %copy-done.4, ...), custom_call_target="tpu_custom_call" | custom-call | tf_op jit(solution)/shard_map/pallas_call | solution.py:493
  62.1 0.0 copy-done.1
  62.2 6.1 %shard_map.88 = f32[2,512,512]{2,1,0:T(8,128)} custom-call(s32[8,2]{1,0:T(8,128)S(1)} %copy.10.pos, f32[2,512,512]{2,1,0:T(8,128)S(1)} %copy-done.1, f32[8,2,256,256]{3,2,1,0:T(8,128)S(1)} %get-tuple-element.9.grad, f32[256,256]{1,0:T(8,128)S(1)} %get-tuple-element.10.light), custom_call_target="tpu_custom_call" | custom-call | tf_op jit(solution)/shard_map/pallas_call | solution.py:522
  68.3 0.8 %copy.13 = f32[1,2,256,256]{3,2,1,0:T(8,128)} copy(f32[1,2,256,256]{3,2,1,0:T(8,128)S(1)} %get-tuple-element.15) | data formatting | bytes 1048576
Async XLA Ops:
  2.0 1.6 %copy-start = (f32[2,512,512]{2,1,0:T(8,128)S(1)}, f32[2,512,512]{2,1,0:T(8,128)}, u32[]{:S(2)}) copy-start(f32[2,512,512]{2,1,0:T(8,128)} %obj.3) | copy-start | bytes 6291460
  3.6 4.2 %copy-start.2 = (f32[1,1,8,256,256]{4,3,2,1,0:T(8,128)S(1)}, f32[1,1,8,256,256]{4,3,2,1,0:T(8,128)}, u32[]{:S(2)}) copy-start(f32[1,1,8,256,256]{4,3,2,1,0:T(8,128)} %param.9) | copy-start | bytes 6291460
  7.9 1.2 %copy-start.3 = (bf16[4,2,256,256]{3,2,1,0:T(8,128)(2,1)S(1)}, bf16[4,2,256,256]{3,2,1,0:T(8,128)(2,1)}, u32[]{:S(2)}) copy-start(bf16[4,2,256,256]{3,2,1,0:T(8,128)(2,1)} %constant.4.clone.table) | copy-start | bytes 3145732
  9.1 1.0 %copy-start.4 = (f32[1,2,256,256]{3,2,1,0:T(8,128)S(1)}, f32[1,2,256,256]{3,2,1,0:T(8,128)}, u32[]{:S(2)}) copy-start(f32[1,2,256,256]{3,2,1,0:T(8,128)} %probes.1) | copy-start | bytes 1572868
  10.1 0.9 %copy-start.5 = (bf16[2,256,256]{2,1,0:T(8,128)(2,1)S(1)}, bf16[2,256,256]{2,1,0:T(8,128)(2,1)}, u32[]{:S(2)}) copy-start(bf16[2,256,256]{2,1,0:T(8,128)(2,1)} %constant.5.clone.order) | copy-start | bytes 786436
  11.1 51.1 %copy-start.1 = (f32[2,512,512]{2,1,0:T(8,128)S(1)}, f32[2,512,512]{2,1,0:T(8,128)}, u32[]{:S(2)}) copy-start(f32[2,512,512]{2,1,0:T(8,128)} %obj.3) | copy-start | bytes 6291460
